TPU v7x, 128 devices: a whole 4x4x4 slice. The times are simulated.
128 devices in a mesh: dp: 2 (over core), row: 4 (over x), col: 16 (over z, y).
Axes of the slice: x: 4, y: 4, z: 4, core: 2. Of those that a mesh axis runs over, the one named last changes fastest.
Arguments:
- forget_tokens: bfloat16 [256, 6144], P('dp', 'col'), may hold values from -6 to 6
- forget_cotangent: bfloat16 [256, 6144], P('dp', 'col'), may hold values from -6 to 6
- forget_labels: int32 [256], P('dp'), may hold values 0 or 1
- retain_tokens: bfloat16 [256, 6144], P('dp', 'col'), may hold values from -6 to 6
- ln_gain: float32 [6144], P('col'), may hold values from 0.25 to 1.75
- w_in: bfloat16 [6144, 24576], P('col', 'row'), may hold values from -0.078125 to 0.078125
- b_in: float32 [24576], P('row'), may hold values from -3 to 3
- w_out: bfloat16 [24576, 6144], P('row', 'col'), may hold values from -0.0390625 to 0.0390625
- b_out: float32 [6144], P('col'), may hold values from -3 to 3
- pruned: int32 [512], P('row'), may hold values from 0 to 24575, as said below
Outputs:
- saliency: float32 [24576], P('row')
- retain_out: bfloat16 [256, 6144], P(('dp', 'row'), 'col')
Inputs may be any that keep to these rules, and one draw needn't show every extreme that they name: `pruned`: entries r * 128 to (r + 1) * 128 - 1 are distinct neurons that all lie in the r-th of the equal neuron ranges of the row shards.
All inputs are finite; a program needn't handle non-finite values. No bound on the sum of `forget_labels` on one device may be relied on, other than what follows from the above.
Results may differ from a plain program's by a relative error of at most 0.0052.
Values may be sent and summed in bfloat16 or wider, within the bound.
No kernel may reach another device: no remote copies, remote signals or barrier semaphores. Data moves between devices by JAX's collectives and lax.ppermute only.
A program may use at most 128 MiB of HBM per device.

v0:
```python
import jax
import jax.numpy as jnp
from jax import lax
from jax.sharding import PartitionSpec as P

D = 6144


def gelu_exact(v):
    return v * 0.5 * (1.0 + lax.erf(v * 0.7071067811865476))


def gelu_slope(v):
    return (
        0.5 * (1.0 + lax.erf(v * 0.7071067811865476))
        + v * jnp.exp(-0.5 * v * v) * 0.3989422804014327
    )


def outer_rows(left, right):
    return lax.dot_general(
        left, right, (((0,), (0,)), ((), ())), preferred_element_type=jnp.float32
    )


def local(
    forget_tokens,
    forget_cotangent,
    forget_labels,
    retain_tokens,
    ln_gain,
    w_in,
    b_in,
    w_out,
    b_out,
    pruned,
):
    forget_rows = forget_tokens.shape[0]
    width_local = w_in.shape[0]
    neurons_local = w_in.shape[1]
    joined = jnp.concatenate([forget_tokens, retain_tokens], axis=0).astype(jnp.float32)
    mean_val = lax.psum(jnp.sum(joined, axis=1, keepdims=True), "col") / D
    centred = joined - mean_val
    var_val = lax.psum(jnp.sum(centred * centred, axis=1, keepdims=True), "col") / D
    normed = (centred * lax.rsqrt(var_val + 1e-06) * ln_gain).astype(jnp.bfloat16)
    partial_pre = jnp.dot(normed, w_in, preferred_element_type=jnp.float32)
    grad_y = forget_cotangent * forget_labels[:, None].astype(jnp.bfloat16)
    grad_part = lax.dot_general(
        grad_y, w_out, (((1,), (1,)), ((), ())), preferred_element_type=jnp.float32
    )
    share_width = neurons_local // lax.axis_size("col")
    share_start = lax.axis_index("col") * share_width
    bias_share = lax.dynamic_slice_in_dim(b_in, share_start, share_width, 0)
    pre_share = lax.psum_scatter(partial_pre, "col", scatter_dimension=1, tiled=True) + bias_share
    act_share = gelu_exact(pre_share).astype(jnp.bfloat16)
    act_all = lax.all_gather(act_share, "col", axis=1, tiled=True)
    grad_act_share = lax.psum_scatter(
        grad_part.astype(jnp.bfloat16), "col", scatter_dimension=1, tiled=True
    ).astype(jnp.float32)
    grad_pre_share = (grad_act_share * gelu_slope(pre_share[:forget_rows])).astype(jnp.bfloat16)
    grad_pre = lax.all_gather(grad_pre_share, "col", axis=1, tiled=True)
    act_f = act_all[:forget_rows]
    act_r = act_all[forget_rows:]
    normed_f = normed[:forget_rows]
    local_in = outer_rows(normed_f, grad_pre)
    local_out = outer_rows(act_f, grad_y)
    summed_in, summed_out = (
        lax.psum_scatter(
            local_in.astype(jnp.bfloat16), "dp", scatter_dimension=0, tiled=True
        ).astype(jnp.float32),
        lax.psum_scatter(
            local_out.astype(jnp.bfloat16), "dp", scatter_dimension=1, tiled=True
        ).astype(jnp.float32),
    )
    slice_rows = width_local // lax.axis_size("dp")
    slice_start = lax.axis_index("dp") * slice_rows
    weight_in_rows = lax.dynamic_slice_in_dim(w_in, slice_start, slice_rows, 0).astype(jnp.float32)
    weight_out_cols = lax.dynamic_slice_in_dim(w_out, slice_start, slice_rows, 1).astype(
        jnp.float32
    )
    terms = jnp.sum(jnp.abs(weight_in_rows * summed_in), axis=0) + jnp.sum(
        jnp.abs(weight_out_cols * summed_out), axis=1
    )
    saliency = lax.psum(terms, ("dp", "col")) / D
    neuron_ids = lax.axis_index("row") * neurons_local + jnp.arange(neurons_local, dtype=jnp.int32)
    is_pruned = jnp.any(pruned[:, None] == neuron_ids[None, :], axis=0)
    keep = jnp.where(is_pruned, 0.0, 1.0).astype(jnp.bfloat16)
    masked_r = act_r * keep[None, :]
    out_part = jnp.dot(masked_r, w_out, preferred_element_type=jnp.float32)
    retain_out = (
        lax.psum_scatter(out_part, "row", scatter_dimension=0, tiled=True) + b_out
    ).astype(jnp.bfloat16)
    return (saliency, retain_out)


def solution(mesh):
    in_specs = (
        P("dp", "col"),
        P("dp", "col"),
        P("dp"),
        P("dp", "col"),
        P("col"),
        P("col", "row"),
        P("row"),
        P("row", "col"),
        P("col"),
        P("row"),
    )
    out_specs = (P("row"), P(("dp", "row"), "col"))
    return jax.shard_map(local, mesh=mesh, in_specs=in_specs, out_specs=out_specs, check_vma=False)
```

profile of v0, /device:TPU:1, one launch (start us, length us, event | category | flops | bytes accessed | tf_op | source)
XLA Modules:
  0.0 550.1 jit_solution(13570674265357662978)
XLA Ops:
  7.2 0.0 reduce-scatter.8.cloned.1.call-start
  7.2 1.1 convert_reduce_fusion
  8.3 35.5 %psum.21 = f32[256,1]{0,1:T(1,128)S(1)} all-reduce(f32[256,1]{0,1:T(1,128)S(1)} %bitcast.16), channel_id=1, replica_groups=mesh['dp'=2,'row'=4,'col'=16] {'col'}, use_global_device_ids=true, to_apply=%region_1.0 | all-reduce | flops 256 | bytes 2048 | tf_op jit(solution)/shard_map/psum | solution.py:42
  43.8 1.1 fusion.5
  44.9 28.5 %psum.22 = f32[256,1]{0,1:T(1,128)S(1)} all-reduce(f32[256,1]{0,1:T(1,128)S(1)} %bitcast.17), channel_id=1, replica_groups=mesh['dp'=2,'row'=4,'col'=16] {'col'}, use_global_device_ids=true, to_apply=%region_3.0 | all-reduce | flops 256 | bytes 2048 | tf_op jit(solution)/shard_map/psum | solution.py:44
  73.5 1.1 fusion.7
  74.6 6.8 %fusion.19 = f32[256,6144]{1,0:T(8,128)} fusion(bf16[256,384]{1,0:T(8,128)(2,1)S(1)} %fusion.7, bf16[384,6144]{1,0:T(8,128)(2,1)} %param.15), kind=kOutput, calls=%fused_computation.39 | convolution fusion | flops 1207959552 | bytes 11206656 | tf_op jit(solution)/shard_map/dot_general | solution.py:46
  81.4 0.0 copy-start.5
  81.4 0.0 copy-start.2
  81.4 0.0 reduce-scatter.8.cloned.1.call-update
  81.4 0.0 reduce-scatter.16.cloned.1.call-start
  81.4 0.6 copy-done.5
  82.0 0.2 copy-done.2
  82.3 3.9 convolution_convert_fusion.2
  86.2 0.0 copy-start.4
  86.2 1.7 copy.16
  87.9 0.0 reduce-scatter.16.cloned.1.call-update
  87.9 0.0 all-gather.5.cloned.1.call-start
  88.0 0.8 dynamic_slice.10
  88.8 85.5 %reduce-scatter.8.cloned.1.call-done = f32[256,384]{1,0:T(8,128)} async-done(((f32[256,6144]{1,0:T(8,128)}), f32[256,384]{1,0:T(8,128)}) %reduce-scatter.8.cloned.1.call-update) | async-done | bytes 393232 | tf_op jit(solution)/shard_map/reduce_scatter | solution.py:54
  174.2 1.8 multiply_convert_fusion
  176.0 0.0 all-gather.5.cloned.1.call-update
  176.0 0.0 all-gather.3.cloned.1.call-start
  176.1 73.9 %reduce-scatter.16.cloned.1.call-done = bf16[384,128]{1,0:T(8,128)(2,1)} async-done(((bf16[6144,128]{1,0:T(8,128)(2,1)}), bf16[384,128]{1,0:T(8,128)(2,1)}) %reduce-scatter.16.cloned.1.call-update) | async-done | bytes 98320
  249.9 1.0 copy.17
  250.9 0.7 fusion.13
  251.7 0.0 all-gather.3.cloned.1.call-update
  251.7 0.0 reduce-scatter.14.cloned.1.call-start
  251.7 0.0 copy-done.4
  251.8 0.5 compare_reduce_fusion
  252.3 52.4 %all-gather.5.cloned.1.call-done = bf16[256,6144]{1,0:T(8,128)(2,1)} async-done(((bf16[256,384]{1,0:T(8,128)(2,1)}), bf16[256,6144]{1,0:T(8,128)(2,1)}) %all-gather.5.cloned.1.call-update) | async-done | bytes 3145744 | tf_op jit(solution)/shard_map/all_gather | solution.py:56
  304.7 4.5 fusion
  309.2 0.0 reduce-scatter.14.cloned.1.call-update
  309.2 0.0 reduce-scatter.10.cloned.1.call-start
  309.3 41.8 %all-gather.3.cloned.1.call-done = bf16[128,6144]{1,0:T(8,128)(2,1)} async-done(((bf16[128,384]{1,0:T(8,128)(2,1)}), bf16[128,6144]{1,0:T(8,128)(2,1)}) %all-gather.3.cloned.1.call-update) | async-done | bytes 1572880 | tf_op jit(solution)/shard_map/all_gather | solution.py:61
  351.1 4.9 convolution_convert_fusion.1
  356.0 0.0 copy-start.1
  356.0 0.0 reduce-scatter.10.cloned.1.call-update
  356.1 0.0 reduce-scatter.12.cloned.1.call-start
  356.1 1.8 copy-done.1
  357.9 3.7 convolution_convert_fusion
  361.6 0.0 reduce-scatter.12.cloned.1.call-update
  361.6 3.6 constant_dynamic-slice_fusion
  365.2 0.0 copy-start.3
  365.2 2.7 copy.18
  367.9 0.0 copy-start
  367.9 4.1 reduce-scatter.14.cloned.1.call-done
  372.0 0.0 copy-done.3
  372.0 1.4 add_convert_fusion
  373.4 18.7 %reduce-scatter.10.cloned.1.call-done = bf16[192,6144]{1,0:T(8,128)(2,1)} async-done(((bf16[384,6144]{1,0:T(8,128)(2,1)}), bf16[192,6144]{1,0:T(8,128)(2,1)}) %reduce-scatter.10.cloned.1.call-update) | async-done | bytes 2359312 | tf_op jit(solution)/shard_map/reduce_scatter | solution.py:68
  392.2 3.2 abs_reduce_fusion.1
  395.3 15.9 %reduce-scatter.12.cloned.1.call-done = bf16[6144,192]{0,1:T(8,128)(2,1)} async-done(((bf16[6144,384]{0,1:T(8,128)(2,1)}), bf16[6144,192]{0,1:T(8,128)(2,1)}) %reduce-scatter.12.cloned.1.call-update) | async-done | bytes 2359312 | tf_op jit(solution)/shard_map/reduce_scatter | solution.py:71
  411.2 0.0 copy-done
  411.2 2.5 abs_reduce_fusion
  413.7 128.9 %psum.23 = f32[6144]{0:T(1024)S(1)} all-reduce(f32[6144]{0:T(1024)S(1)} %add.84), channel_id=1, replica_groups=mesh['dp'=2,'row'=4,'col'=16] {'dp','col'}, use_global_device_ids=true, to_apply=%region_10.0 | all-reduce | flops 6144 | bytes 49152 | tf_op jit(solution)/shard_map/psum | solution.py:84
  542.6 0.6 broadcast_multiply_fusion
  (6 shorter events, 0.0 us)
Async XLA Ops:
  7.2 167.1 %reduce-scatter.8.cloned.1.call-start = ((), (), s32[]{:S(2)}) async-start(), calls=%async_computation.5 | async-start | bytes 6684672 | tf_op jit(solution)/shard_map/reduce_scatter | solution.py:54
  81.4 0.7 copy-start.5
  81.4 0.9 copy-start.2
  81.4 168.5 %reduce-scatter.16.cloned.1.call-start = ((), (), s32[]{:S(2)}) async-start(), calls=%async_computation.11 | async-start | bytes 1671168
  86.2 165.5 %copy-start.4 = (s32[128]{0:T(128)S(1)}, s32[128]{0:T(128)}, u32[]{:S(2)}) copy-start(s32[128]{0:T(128)} %param.19) | copy-start | bytes 1540
  87.9 216.8 %all-gather.5.cloned.1.call-start = ((), (), s32[]{:S(2)}) async-start(), calls=%async_computation.8 | async-start | bytes 3342336 | tf_op jit(solution)/shard_map/all_gather | solution.py:56
  176.0 175.1 %all-gather.3.cloned.1.call-start = ((), (), s32[]{:S(2)}) async-start(), calls=%async_computation.6 | async-start | bytes 1671168 | tf_op jit(solution)/shard_map/all_gather | solution.py:61
  251.7 120.3 %reduce-scatter.14.cloned.1.call-start = ((), (), s32[]{:S(2)}) async-start(), calls=%async_computation.10 | async-start | bytes 245760 | tf_op jit(solution)/shard_map/reduce_scatter | solution.py:91
  309.2 82.9 %reduce-scatter.10.cloned.1.call-start = ((), (), s32[]{:S(2)}) async-start(), calls=%async_computation.7 | async-start | bytes 7077888 | tf_op jit(solution)/shard_map/reduce_scatter | solution.py:68
  356.0 1.9 copy-start.1
  356.1 55.2 %reduce-scatter.12.cloned.1.call-start = ((), (), s32[]{:S(2)}) async-start(), calls=%async_computation.9 | async-start | bytes 7077888 | tf_op jit(solution)/shard_map/reduce_scatter | solution.py:71
  365.2 6.9 %copy-start.3 = (f32[384]{0:T(512)S(1)}, f32[384]{0:T(512)}, u32[]{:S(2)}) copy-start(f32[384]{0:T(512)} %param.18) | copy-start | bytes 4612
  367.9 43.3 %copy-start = (bf16[6144,192]{0,1:T(8,128)(2,1)S(1)}, bf16[6144,192]{0,1:T(8,128)(2,1)}, u32[]{:S(2)}) copy-start(bf16[6144,192]{0,1:T(8,128)(2,1)} %copy.18) | copy-start | bytes 7077892
Sparse Core Ops, SparseCore 0:
  81.5 92.6 reduce-scatter.7
  177.4 72.4 reduce-scatter.15
  252.0 52.6 all-gather.4
  306.7 44.3 all-gather.2
  353.3 18.6 reduce-scatter.13
  374.4 17.6 reduce-scatter.9
  394.6 16.6 reduce-scatter.11
where the time goes:
time: 551 us; the launch traced here: 550 us
  waiting for transfers between devices  292 us (53%)
  blocking collectives  193 us (35%)
  matrix products  23.8 us (4%)
  between operations  14.2 us (3%)
  other arithmetic  14 us (3%)
  local copies, waits for them, and re-layouts  12.4 us (2%)
    psum x1, blocking collectives, local(): saliency = lax.psum(terms, ('dp', 'col')) / D  129 us
    reduce_scatter x1, waiting for transfers between devices, local(): lax.psum_scatter(partial_pre, 'col', scatter_dimension=1, tiled=True)  85.5 us
    unnamed x8, waiting for transfers between devices  74 us
    all_gather x1, waiting for transfers between devices, local(): act_all = lax.all_gather(act_share, 'col', axis=1, tiled=True)  52.4 us
    all_gather x1, waiting for transfers between devices, local(): grad_pre = lax.all_gather(grad_pre_share, 'col', axis=1, tiled=True)  41.8 us
    psum x1, blocking collectives, local(): mean_val = lax.psum(jnp.sum(joined, axis=1, keepdims=True), 'col') / D  35.5 us
    psum x1, blocking collectives, local(): lax.psum(jnp.sum(centred * centred, axis=1, keepdims=True), 'col') / D  28.5 us
    reduce_scatter x1, waiting for transfers between devices, local(): lax.psum_scatter(local_in.astype(jnp.bfloat16), 'dp', scatter_dimension=0...  18.7 us
  transfers between devices with their start and end apart: 7, of which 7 were waited for; matrix products, arithmetic and copies ran while one was open for 6% of the time, Pallas kernels for 0%

commit v1 on v0

--- a/solution.py
+++ b/solution.py
@@ -4,6 +4,11 @@
 from jax.sharding import PartitionSpec as P
 
 D = 6144
+
+
+def one_after_other(value, inner_axis, outer_axis):
+    half = lax.psum(value, inner_axis)
+    return lax.psum(half, outer_axis)
 
 
 def gelu_exact(v):
@@ -81,7 +86,7 @@
     terms = jnp.sum(jnp.abs(weight_in_rows * summed_in), axis=0) + jnp.sum(
         jnp.abs(weight_out_cols * summed_out), axis=1
     )
-    saliency = lax.psum(terms, ("dp", "col")) / D
+    saliency = one_after_other(terms, "col", "dp") / D
     neuron_ids = lax.axis_index("row") * neurons_local + jnp.arange(neurons_local, dtype=jnp.int32)
     is_pruned = jnp.any(pruned[:, None] == neuron_ids[None, :], axis=0)
     keep = jnp.where(is_pruned, 0.0, 1.0).astype(jnp.bfloat16)

time: 551 us -> 500 us (0.907)
  blocking collectives: 193 us -> 142 us
    psum x1 -> x2, blocking collectives: 129 us -> 78.1 us  [the longest x1 60.8 us: one_after_other(): half = lax.psum(value, inner_axis)]
  transfers between devices with their start and end apart: 7 -> 7, of which waited for: 7 -> 7; matrix products, arithmetic and copies ran while one was open for 6% -> 7% of each run, Pallas kernels for 0% -> 0%
where the time goes in v1:
time: 500 us; the launch traced here: 499 us
  waiting for transfers between devices  292 us (58%)
  blocking collectives  142 us (28%)
  matrix products  23.8 us (5%)
  between operations  14.2 us (3%)
  other arithmetic  14 us (3%)
  local copies, waits for them, and re-layouts  12.4 us (2%)
    reduce_scatter x1, waiting for transfers between devices, local(): lax.psum_scatter(partial_pre, 'col', scatter_dimension=1, tiled=True)  85.5 us
    unnamed x8, waiting for transfers between devices  74 us
    psum x1, blocking collectives, one_after_other(): half = lax.psum(value, inner_axis)  60.8 us
    all_gather x1, waiting for transfers between devices, local(): act_all = lax.all_gather(act_share, 'col', axis=1, tiled=True)  52.4 us
    all_gather x1, waiting for transfers between devices, local(): grad_pre = lax.all_gather(grad_pre_share, 'col', axis=1, tiled=True)  41.8 us
    psum x1, blocking collectives, local(): mean_val = lax.psum(jnp.sum(joined, axis=1, keepdims=True), 'col') / D  35.5 us
    psum x1, blocking collectives, local(): lax.psum(jnp.sum(centred * centred, axis=1, keepdims=True), 'col') / D  28.5 us
    reduce_scatter x1, waiting for transfers between devices, local(): lax.psum_scatter(local_in.astype(jnp.bfloat16), 'dp', scatter_dimension=0...  18.7 us
  transfers between devices with their start and end apart: 7, of which 7 were waited for; matrix products, arithmetic and copies ran while one was open for 7% of the time, Pallas kernels for 0%

profile of v1, /device:TPU:1, one launch (start us, length us, event | category | flops | bytes accessed | tf_op | source)
XLA Modules:
  0.0 499.3 jit_solution(684820837986323610)
XLA Ops:
  7.2 0.0 reduce-scatter.8.cloned.1.call-start
  7.2 1.1 convert_reduce_fusion
  8.3 35.5 %psum.28 = f32[256,1]{0,1:T(1,128)S(1)} all-reduce(f32[256,1]{0,1:T(1,128)S(1)} %bitcast.16), channel_id=1, replica_groups=mesh['dp'=2,'row'=4,'col'=16] {'col'}, use_global_device_ids=true, to_apply=%region_1.0 | all-reduce | flops 256 | bytes 2048 | tf_op jit(solution)/shard_map/psum | solution.py:47
  43.8 1.1 fusion.5
  44.9 28.5 %psum.29 = f32[256,1]{0,1:T(1,128)S(1)} all-reduce(f32[256,1]{0,1:T(1,128)S(1)} %bitcast.17), channel_id=1, replica_groups=mesh['dp'=2,'row'=4,'col'=16] {'col'}, use_global_device_ids=true, to_apply=%region_3.0 | all-reduce | flops 256 | bytes 2048 | tf_op jit(solution)/shard_map/psum | solution.py:49
  73.5 1.1 fusion.7
  74.6 6.8 %fusion.19 = f32[256,6144]{1,0:T(8,128)} fusion(bf16[256,384]{1,0:T(8,128)(2,1)S(1)} %fusion.7, bf16[384,6144]{1,0:T(8,128)(2,1)} %param.15), kind=kOutput, calls=%fused_computation.39 | convolution fusion | flops 1207959552 | bytes 11206656 | tf_op jit(solution)/shard_map/dot_general | solution.py:51
  81.4 0.0 copy-start.5
  81.4 0.0 copy-start.2
  81.4 0.0 reduce-scatter.8.cloned.1.call-update
  81.4 0.0 reduce-scatter.16.cloned.1.call-start
  81.4 0.6 copy-done.5
  82.0 0.2 copy-done.2
  82.3 3.9 convolution_convert_fusion.2
  86.2 0.0 copy-start.4
  86.2 1.7 copy.16
  87.9 0.0 reduce-scatter.16.cloned.1.call-update
  87.9 0.0 all-gather.5.cloned.1.call-start
  88.0 0.8 dynamic_slice.10
  88.8 85.5 %reduce-scatter.8.cloned.1.call-done = f32[256,384]{1,0:T(8,128)} async-done(((f32[256,6144]{1,0:T(8,128)}), f32[256,384]{1,0:T(8,128)}) %reduce-scatter.8.cloned.1.call-update) | async-done | bytes 393232 | tf_op jit(solution)/shard_map/reduce_scatter | solution.py:59
  174.2 1.8 multiply_convert_fusion
  176.0 0.0 all-gather.5.cloned.1.call-update
  176.0 0.0 all-gather.3.cloned.1.call-start
  176.1 73.9 %reduce-scatter.16.cloned.1.call-done = bf16[384,128]{1,0:T(8,128)(2,1)} async-done(((bf16[6144,128]{1,0:T(8,128)(2,1)}), bf16[384,128]{1,0:T(8,128)(2,1)}) %reduce-scatter.16.cloned.1.call-update) | async-done | bytes 98320
  249.9 1.0 copy.17
  250.9 0.7 fusion.13
  251.7 0.0 all-gather.3.cloned.1.call-update
  251.7 0.0 reduce-scatter.14.cloned.1.call-start
  251.7 0.0 copy-done.4
  251.8 0.5 compare_reduce_fusion
  252.3 52.4 %all-gather.5.cloned.1.call-done = bf16[256,6144]{1,0:T(8,128)(2,1)} async-done(((bf16[256,384]{1,0:T(8,128)(2,1)}), bf16[256,6144]{1,0:T(8,128)(2,1)}) %all-gather.5.cloned.1.call-update) | async-done | bytes 3145744 | tf_op jit(solution)/shard_map/all_gather | solution.py:61
  304.7 4.5 fusion
  309.2 0.0 reduce-scatter.14.cloned.1.call-update
  309.2 0.0 reduce-scatter.10.cloned.1.call-start
  309.3 41.8 %all-gather.3.cloned.1.call-done = bf16[128,6144]{1,0:T(8,128)(2,1)} async-done(((bf16[128,384]{1,0:T(8,128)(2,1)}), bf16[128,6144]{1,0:T(8,128)(2,1)}) %all-gather.3.cloned.1.call-update) | async-done | bytes 1572880 | tf_op jit(solution)/shard_map/all_gather | solution.py:66
  351.1 4.9 convolution_convert_fusion.1
  356.0 0.0 copy-start.1
  356.0 0.0 reduce-scatter.10.cloned.1.call-update
  356.1 0.0 reduce-scatter.12.cloned.1.call-start
  356.1 1.8 copy-done.1
  357.9 3.7 convolution_convert_fusion
  361.6 0.0 reduce-scatter.12.cloned.1.call-update
  361.6 3.6 constant_dynamic-slice_fusion
  365.2 0.0 copy-start.3
  365.2 2.7 copy.18
  367.9 0.0 copy-start
  367.9 4.1 reduce-scatter.14.cloned.1.call-done
  372.0 0.0 copy-done.3
  372.0 1.4 add_convert_fusion
  373.4 18.7 %reduce-scatter.10.cloned.1.call-done = bf16[192,6144]{1,0:T(8,128)(2,1)} async-done(((bf16[384,6144]{1,0:T(8,128)(2,1)}), bf16[192,6144]{1,0:T(8,128)(2,1)}) %reduce-scatter.10.cloned.1.call-update) | async-done | bytes 2359312 | tf_op jit(solution)/shard_map/reduce_scatter | solution.py:73
  392.2 3.2 abs_reduce_fusion.1
  395.3 15.9 %reduce-scatter.12.cloned.1.call-done = bf16[6144,192]{0,1:T(8,128)(2,1)} async-done(((bf16[6144,384]{0,1:T(8,128)(2,1)}), bf16[6144,192]{0,1:T(8,128)(2,1)}) %reduce-scatter.12.cloned.1.call-update) | async-done | bytes 2359312 | tf_op jit(solution)/shard_map/reduce_scatter | solution.py:76
  411.2 0.0 copy-done
  411.2 2.5 abs_reduce_fusion
  413.7 60.8 %psum.30 = f32[6144]{0:T(1024)S(1)} all-reduce(f32[6144]{0:T(1024)S(1)} %add.86), channel_id=1, replica_groups=mesh['dp'=2,'row'=4,'col'=16] {'col'}, use_global_device_ids=true, to_apply=%region_10.0 | all-reduce | flops 6144 | bytes 49152 | tf_op jit(solution)/shard_map/psum | solution.py:10
  474.5 17.4 %psum.31 = f32[6144]{0:T(1024)S(1)} all-reduce(f32[6144]{0:T(1024)S(1)} %psum.30), channel_id=1, replica_groups=mesh['dp'=2,'row'=4,'col'=16] {'dp'}, use_global_device_ids=true, to_apply=%region_11.0 | all-reduce | flops 6144 | bytes 49152 | tf_op jit(solution)/shard_map/psum | solution.py:11
  491.8 0.6 broadcast_multiply_fusion
  (6 shorter events, 0.0 us)
Async XLA Ops:
  7.2 167.1 %reduce-scatter.8.cloned.1.call-start = ((), (), s32[]{:S(2)}) async-start(), calls=%async_computation.5 | async-start | bytes 6684672 | tf_op jit(solution)/shard_map/reduce_scatter | solution.py:59
  81.4 0.7 copy-start.5
  81.4 0.9 copy-start.2
  81.4 168.5 %reduce-scatter.16.cloned.1.call-start = ((), (), s32[]{:S(2)}) async-start(), calls=%async_computation.11 | async-start | bytes 1671168
  86.2 165.5 %copy-start.4 = (s32[128]{0:T(128)S(1)}, s32[128]{0:T(128)}, u32[]{:S(2)}) copy-start(s32[128]{0:T(128)} %param.19) | copy-start | bytes 1540
  87.9 216.8 %all-gather.5.cloned.1.call-start = ((), (), s32[]{:S(2)}) async-start(), calls=%async_computation.8 | async-start | bytes 3342336 | tf_op jit(solution)/shard_map/all_gather | solution.py:61
  176.0 175.1 %all-gather.3.cloned.1.call-start = ((), (), s32[]{:S(2)}) async-start(), calls=%async_computation.6 | async-start | bytes 1671168 | tf_op jit(solution)/shard_map/all_gather | solution.py:66
  251.7 120.3 %reduce-scatter.14.cloned.1.call-start = ((), (), s32[]{:S(2)}) async-start(), calls=%async_computation.10 | async-start | bytes 245760 | tf_op jit(solution)/shard_map/reduce_scatter | solution.py:96
  309.2 82.9 %reduce-scatter.10.cloned.1.call-start = ((), (), s32[]{:S(2)}) async-start(), calls=%async_computation.7 | async-start | bytes 7077888 | tf_op jit(solution)/shard_map/reduce_scatter | solution.py:73
  356.0 1.9 copy-start.1
  356.1 55.2 %reduce-scatter.12.cloned.1.call-start = ((), (), s32[]{:S(2)}) async-start(), calls=%async_computation.9 | async-start | bytes 7077888 | tf_op jit(solution)/shard_map/reduce_scatter | solution.py:76
  365.2 6.9 %copy-start.3 = (f32[384]{0:T(512)S(1)}, f32[384]{0:T(512)}, u32[]{:S(2)}) copy-start(f32[384]{0:T(512)} %param.18) | copy-start | bytes 4612
  367.9 43.3 %copy-start = (bf16[6144,192]{0,1:T(8,128)(2,1)S(1)}, bf16[6144,192]{0,1:T(8,128)(2,1)}, u32[]{:S(2)}) copy-start(bf16[6144,192]{0,1:T(8,128)(2,1)} %copy.18) | copy-start | bytes 7077892
Sparse Core Ops, SparseCore 0:
  81.5 92.6 reduce-scatter.7
  177.4 72.4 reduce-scatter.15
  252.0 52.6 all-gather.4
  306.7 44.3 all-gather.2
  353.3 18.6 reduce-scatter.13
  374.4 17.6 reduce-scatter.9
  394.6 16.6 reduce-scatter.11
